TPU v7x, 32 devices: a whole 2x2x4 slice. The times are simulated.
32 devices in a mesh: dp: 8 (over y, x, core), tensor: 4 (over z).
Axes of the slice: x: 2, y: 2, z: 4, core: 2. Of those that a mesh axis runs over, the one named last changes fastest.
Arguments:
- block_input: float32 [12544, 512], P(('dp', 'tensor')), as said below
- cotangent: float32 [12544, 512], P(('dp', 'tensor')), may hold values from -6 to 6
- w_qkv: bfloat16 [2, 512, 3, 512], P(None, 'dp', None, 'tensor'), may hold values from -0.25 to 0.25
- b_qv: bfloat16 [2, 2, 512], P(None, None, 'tensor'), may hold values from -3 to 3
- bias_table: bfloat16 [2, 169, 16], P(None, None, 'tensor'), may hold values from -4 to 4
- w_proj: bfloat16 [2, 512, 512], P(None, 'tensor', 'dp'), may hold values from -0.75 to 0.75
- w_fc1: bfloat16 [2, 512, 2048], P(None, 'dp', 'tensor'), may hold values from -0.25 to 0.25
- b_fc1: bfloat16 [2, 2048], P(None, 'tensor'), may hold values from -3 to 3
- w_fc2: bfloat16 [2, 2048, 512], P(None, 'tensor', 'dp'), may hold values from -0.1875 to 0.1875
- norm_params: bfloat16 [2, 6, 512], P(None, None, 'dp'), as said below
- rel_index: int32 [49, 49], replicated, may hold values from 0 to 168, as said below
- shift_perm: int32 [196], replicated, may hold values from 0 to 195, as said below
- shift_mask: int32 [4, 49, 49], replicated, may hold values from 0 to 1, as said below
Outputs:
- block_output: float32 [12544, 512], P(('dp', 'tensor'))
- d_block_input: float32 [12544, 512], P(('dp', 'tensor'))
- d_w_qkv: float32 [2, 512, 3, 512], P(None, 'dp', None, 'tensor')
- d_b_qv: float32 [2, 2, 512], P(None, None, 'tensor')
- d_bias_table: float32 [2, 169, 16], P(None, None, 'tensor')
- d_w_proj: float32 [2, 512, 512], P(None, 'tensor', 'dp')
- d_w_fc1: float32 [2, 512, 2048], P(None, 'dp', 'tensor')
- d_b_fc1: float32 [2, 2048], P(None, 'tensor')
- d_w_fc2: float32 [2, 2048, 512], P(None, 'tensor', 'dp')
- d_norm_params: float32 [2, 6, 512], P(None, None, 'dp')
Inputs may be any that keep to these rules, and one draw needn't show every extreme that they name: `block_input`: standard normal scaled by a factor per token and a factor per feature. `norm_params`: rows 0 and 3 are positive gains. `rel_index`: two pairs of window positions have equal entries exactly when they have the same row offset and the same column offset; every value appears. A permutation: the image is rolled cyclically by amounts of 1 to 6 tokens, drawn once, along both grid dimensions, and cut into windows; window-ordered position j of the rolled image holds the token whose window-ordered position is shift_perm[j]. `shift_mask`: 1 where two positions of a window of the rolled image of shift_perm lie in different regions of the shifted-window partition for that roll, else 0; zero on the diagonal.
All inputs are finite; a program needn't handle non-finite values.
Results may differ from a plain program's by a relative error of at most 0.022.
Values may be sent and summed in bfloat16 or wider, within the bound.
No kernel may reach another device: no remote copies, remote signals or barrier semaphores. Data moves between devices by JAX's collectives and lax.ppermute only.
A program may use at most 192 MiB of HBM per device.

v0:
```python
import jax
import jax.numpy as jnp
from jax import lax
from jax.sharding import PartitionSpec as P

D = 512
HEAD_DIM = 32
WTOK = 49
ITOK = 196
NWIN = 4
RELS = 169
EPS = 1e-05
MASKED = -100.0
ROOT_HALF = 0.7071067811865476
ROOT_TWO_PI = 2.5066282746310002
full_precision = lax.Precision.HIGHEST


def gelu_value(inputs):
    return inputs * 0.5 * (1.0 + lax.erf(inputs * ROOT_HALF))


def gelu_slope(inputs):
    return (
        0.5 * (1.0 + lax.erf(inputs * ROOT_HALF))
        + inputs * jnp.exp(-0.5 * inputs * inputs) / ROOT_TWO_PI
    )


def layer_norm(hidden, norm_gain, offset):
    row_mean = jnp.mean(hidden, axis=-1, keepdims=True)
    centred = hidden - row_mean
    inv_std = lax.rsqrt(jnp.mean(centred * centred, axis=-1, keepdims=True) + EPS)
    normed = centred * inv_std
    return (normed * norm_gain + offset, normed, inv_std)


def norm_back(grad_rows, normed, inv_std, norm_gain):
    scaled = grad_rows * norm_gain
    centred_grad = (
        scaled
        - jnp.mean(scaled, axis=-1, keepdims=True)
        - normed * jnp.mean(scaled * normed, axis=-1, keepdims=True)
    )
    return inv_std * centred_grad


def inner_rows(left_side, right_side):
    return lax.dot_general(
        left_side, right_side, (((0,), (0,)), ((), ())), preferred_element_type=jnp.float32
    )


def times_transposed(left_side, right_side):
    return lax.dot_general(
        left_side, right_side, (((1,), (1,)), ((), ())), preferred_element_type=jnp.float32
    )


def rel_lookup(rel_index):
    flat_cells = rel_index.reshape(-1)
    return (flat_cells[:, None] == jnp.arange(RELS, dtype=jnp.int32)[None, :]).astype(jnp.float32)


def position_bias(lookup, pos_table):
    head_count = pos_table.shape[-1]
    flat_bias = jnp.dot(lookup, pos_table.astype(jnp.float32), precision=full_precision)
    return flat_bias.reshape(WTOK, WTOK, head_count).transpose(2, 0, 1)


def window_scores(query_blocks, key_blocks, pos_bias, mask_term):
    scores = jnp.einsum(
        "inqhe,inkhe->inhqk", query_blocks, key_blocks, preferred_element_type=jnp.float32
    )
    scores = scores + pos_bias[None, None]
    if mask_term is not None:
        scores = scores + mask_term[None, :, None]
    return scores


def spread_rows(values):
    return lax.all_gather(values, "tensor", axis=0, tiled=True)


def spread_grads(values):
    return lax.all_gather(values, "tensor", axis=0, tiled=True)


def branch_sum(values, weight):
    return lax.psum_scatter(
        jnp.dot(values, weight, preferred_element_type=jnp.float32).astype(jnp.bfloat16),
        "tensor",
        scatter_dimension=0,
        tiled=True,
    ).astype(jnp.float32)


def back_sum(values, weight):
    return lax.psum_scatter(
        times_transposed(values, weight).astype(jnp.bfloat16),
        "tensor",
        scatter_dimension=0,
        tiled=True,
    ).astype(jnp.float32)


def forward_layer(hidden, weights, lookup, mask_term, reorder):
    w_qkv, b_qv, pos_table, w_proj, w_fc1, b_fc1, w_fc2, norm_rows = weights
    norm_rows = norm_rows.astype(jnp.float32)
    local_width = w_qkv.shape[-1]
    head_count = local_width // HEAD_DIM
    score_scale = HEAD_DIM ** (-0.5)
    ln_first, normed_first, inv_first = layer_norm(hidden, norm_rows[0], norm_rows[1])
    gathered = spread_rows(ln_first.astype(jnp.bfloat16))
    image_count = gathered.shape[0] // ITOK
    arranged = gathered.reshape(image_count, ITOK, D)
    if reorder is not None:
        arranged = jnp.take(arranged, reorder[0], axis=1)
    permuted_rows = arranged.reshape(image_count * ITOK, D)
    projected = jnp.dot(
        permuted_rows, w_qkv.reshape(D, 3 * local_width), preferred_element_type=jnp.float32
    )
    projected = projected.reshape(-1, 3, local_width)
    biases = b_qv.astype(jnp.float32)
    query_rows = ((projected[:, 0] + biases[0]) * score_scale).astype(jnp.bfloat16)
    key_rows = projected[:, 1].astype(jnp.bfloat16)
    value_rows = (projected[:, 2] + biases[1]).astype(jnp.bfloat16)
    block_shape = (image_count, NWIN, WTOK, head_count, HEAD_DIM)
    query_blocks = query_rows.reshape(block_shape)
    key_blocks = key_rows.reshape(block_shape)
    value_blocks = value_rows.reshape(block_shape)
    pos_bias = position_bias(lookup, pos_table)
    scores = window_scores(query_blocks, key_blocks, pos_bias, mask_term)
    row_peak = jnp.max(scores, axis=-1, keepdims=True)
    log_total = row_peak + jnp.log(jnp.sum(jnp.exp(scores - row_peak), axis=-1, keepdims=True))
    soft_weights = jnp.exp(scores - log_total).astype(jnp.bfloat16)
    mixed = jnp.einsum(
        "inhqk,inkhe->inqhe", soft_weights, value_blocks, preferred_element_type=jnp.float32
    ).astype(jnp.bfloat16)
    mixed = mixed.reshape(image_count, ITOK, local_width)
    if reorder is not None:
        mixed = jnp.take(mixed, reorder[1], axis=1)
    mixed = mixed.reshape(image_count * ITOK, local_width)
    residual = hidden + branch_sum(mixed, w_proj) + norm_rows[2]
    ln_second, normed_second, inv_second = layer_norm(residual, norm_rows[3], norm_rows[4])
    spread = spread_rows(ln_second.astype(jnp.bfloat16))
    pre_active = jnp.dot(spread, w_fc1, preferred_element_type=jnp.float32) + b_fc1.astype(
        jnp.float32
    )
    active = gelu_value(pre_active).astype(jnp.bfloat16)
    result = residual + branch_sum(active, w_fc2) + norm_rows[5]
    kept_state = (
        normed_first,
        inv_first,
        permuted_rows,
        query_blocks,
        key_blocks,
        value_blocks,
        log_total,
        mixed,
        normed_second,
        inv_second,
        spread,
        pre_active,
        active,
    )
    return (result, kept_state)


def backward_layer(out_grad, kept_state, weights, lookup, mask_term, reorder):
    (
        normed_first,
        inv_first,
        permuted_rows,
        query_blocks,
        key_blocks,
        value_blocks,
        log_total,
        mixed,
        normed_second,
        inv_second,
        spread,
        pre_active,
        active,
    ) = kept_state
    w_qkv, b_qv, pos_table, w_proj, w_fc1, b_fc1, w_fc2, norm_rows = weights
    norm_rows = norm_rows.astype(jnp.float32)
    local_width = w_qkv.shape[-1]
    head_count = local_width // HEAD_DIM
    score_scale = HEAD_DIM ** (-0.5)
    image_count = permuted_rows.shape[0] // ITOK
    grad_rounded = spread_grads(out_grad.astype(jnp.bfloat16))
    d_fc2 = inner_rows(active, grad_rounded)
    d_active = times_transposed(grad_rounded, w_fc2)
    d_pre = d_active * gelu_slope(pre_active)
    d_bias_fc1 = jnp.sum(d_pre, axis=0)
    d_pre_rounded = d_pre.astype(jnp.bfloat16)
    d_fc1 = inner_rows(spread, d_pre_rounded)
    d_spread = back_sum(d_pre_rounded, w_fc1)
    d_residual = out_grad + norm_back(d_spread, normed_second, inv_second, norm_rows[3])
    mix_grad = spread_grads(d_residual.astype(jnp.bfloat16))
    d_proj = inner_rows(mixed, mix_grad)
    d_mixed = (
        times_transposed(mix_grad, w_proj)
        .astype(jnp.bfloat16)
        .reshape(image_count, ITOK, local_width)
    )
    if reorder is not None:
        d_mixed = jnp.take(d_mixed, reorder[0], axis=1)
    d_mixed_blocks = d_mixed.reshape(image_count, NWIN, WTOK, head_count, HEAD_DIM)
    pos_bias = position_bias(lookup, pos_table)
    scores = window_scores(query_blocks, key_blocks, pos_bias, mask_term)
    soft_exact = jnp.exp(scores - log_total)
    d_values = jnp.einsum(
        "inhqk,inqhe->inkhe",
        soft_exact.astype(jnp.bfloat16),
        d_mixed_blocks,
        preferred_element_type=jnp.float32,
    )
    d_soft = jnp.einsum(
        "inqhe,inkhe->inhqk", d_mixed_blocks, value_blocks, preferred_element_type=jnp.float32
    )
    d_scores = soft_exact * (d_soft - jnp.sum(soft_exact * d_soft, axis=-1, keepdims=True))
    score_total = jnp.sum(d_scores, axis=(0, 1)).reshape(head_count, WTOK * WTOK)
    d_table = jnp.dot(lookup.T, score_total.T, precision=full_precision)
    d_scores_rounded = d_scores.astype(jnp.bfloat16)
    d_query = (
        jnp.einsum(
            "inhqk,inkhe->inqhe", d_scores_rounded, key_blocks, preferred_element_type=jnp.float32
        )
        * score_scale
    )
    d_keys = jnp.einsum(
        "inhqk,inqhe->inkhe", d_scores_rounded, query_blocks, preferred_element_type=jnp.float32
    )
    d_query = d_query.reshape(-1, local_width)
    d_keys = d_keys.reshape(-1, local_width)
    d_values = d_values.reshape(-1, local_width)
    d_bias_qv = jnp.stack([jnp.sum(d_query, axis=0), jnp.sum(d_values, axis=0)])
    d_joint = (
        jnp.stack([d_query, d_keys, d_values], axis=1)
        .astype(jnp.bfloat16)
        .reshape(-1, 3 * local_width)
    )
    d_qkv = inner_rows(permuted_rows, d_joint).reshape(D, 3, local_width)
    if reorder is not None:
        d_joint = jnp.take(
            d_joint.reshape(image_count, ITOK, 3 * local_width), reorder[1], axis=1
        ).reshape(image_count * ITOK, 3 * local_width)
    d_normed = back_sum(d_joint, w_qkv.reshape(D, 3 * local_width))
    d_hidden = d_residual + norm_back(d_normed, normed_first, inv_first, norm_rows[0])
    norm_grads = jnp.stack(
        [
            jnp.sum(d_normed * normed_first, axis=0),
            jnp.sum(d_normed, axis=0),
            jnp.sum(d_residual, axis=0),
            jnp.sum(d_spread * normed_second, axis=0),
            jnp.sum(d_spread, axis=0),
            jnp.sum(out_grad, axis=0),
        ]
    )
    return (d_hidden, (d_qkv, d_proj, d_fc1, d_fc2), (d_bias_qv, d_table, d_bias_fc1), norm_grads)


def join_two(first_item, second_item):
    return jnp.concatenate([first_item, second_item], axis=0)


def body(
    block_input,
    cotangent,
    w_qkv,
    b_qv,
    bias_table,
    w_proj,
    w_fc1,
    b_fc1,
    w_fc2,
    norm_params,
    rel_index,
    shift_perm,
    shift_mask,
):
    full_qkv, full_proj, full_fc1, full_fc2, norm_rows = (
        lax.all_gather(w_qkv, "dp", axis=1, tiled=True),
        lax.all_gather(w_proj, "dp", axis=2, tiled=True),
        lax.all_gather(w_fc1, "dp", axis=1, tiled=True),
        lax.all_gather(w_fc2, "dp", axis=2, tiled=True),
        lax.all_gather(norm_params, "dp", axis=2, tiled=True),
    )
    head_bias, pos_table, fc1_bias = (b_qv, bias_table, b_fc1)
    inverse = jnp.zeros((ITOK,), jnp.int32).at[shift_perm].set(jnp.arange(ITOK, dtype=jnp.int32))
    reorder = (shift_perm, inverse)
    lookup = rel_lookup(rel_index)
    mask_term = shift_mask.astype(jnp.float32) * MASKED

    def weights_of(layer_index):
        return (
            full_qkv[layer_index],
            head_bias[layer_index],
            pos_table[layer_index],
            full_proj[layer_index],
            full_fc1[layer_index],
            fc1_bias[layer_index],
            full_fc2[layer_index],
            norm_rows[layer_index],
        )

    first_out, kept_first = forward_layer(block_input, weights_of(0), lookup, None, None)
    second_out, kept_second = forward_layer(first_out, weights_of(1), lookup, mask_term, reorder)
    kept_layers = (kept_first, kept_second)
    layer_masks = (None, mask_term)
    layer_orders = (None, reorder)
    grad_now = cotangent
    finished = []
    for layer_index in (1, 0):
        grad_now, weight_grads, small_grads, norm_grads = backward_layer(
            grad_now,
            kept_layers[layer_index],
            weights_of(layer_index),
            lookup,
            layer_masks[layer_index],
            layer_orders[layer_index],
        )
        d_qkv, d_proj, d_fc1, d_fc2 = weight_grads
        d_bias_qv, d_table, d_bias_fc1 = small_grads
        norm_sum = lax.psum(norm_grads, "tensor")
        shards = (d_qkv[None], d_proj[None], d_fc1[None], d_fc2[None], norm_sum[None])
        finished.append((shards, (d_bias_qv[None], d_table[None], d_bias_fc1[None])))
    later_layer = finished[0]
    earlier_layer = finished[1]
    joined_qkv, joined_proj, joined_fc1, joined_fc2, joined_norms = jax.tree.map(
        join_two, earlier_layer[0], later_layer[0]
    )
    small_qv, small_table, small_fc1 = jax.tree.map(join_two, earlier_layer[1], later_layer[1])
    joined_qkv, joined_proj, joined_fc1, joined_fc2, joined_norms = (
        lax.psum_scatter(
            joined_qkv.astype(jnp.bfloat16), "dp", scatter_dimension=1, tiled=True
        ).astype(jnp.float32),
        lax.psum_scatter(
            joined_proj.astype(jnp.bfloat16), "dp", scatter_dimension=2, tiled=True
        ).astype(jnp.float32),
        lax.psum_scatter(
            joined_fc1.astype(jnp.bfloat16), "dp", scatter_dimension=1, tiled=True
        ).astype(jnp.float32),
        lax.psum_scatter(
            joined_fc2.astype(jnp.bfloat16), "dp", scatter_dimension=2, tiled=True
        ).astype(jnp.float32),
        lax.psum_scatter(
            joined_norms.astype(jnp.bfloat16), "dp", scatter_dimension=2, tiled=True
        ).astype(jnp.float32),
    )
    d_bias_qv, d_table, d_bias_fc1 = lax.psum((small_qv, small_table, small_fc1), "dp")
    return (
        second_out,
        grad_now,
        joined_qkv,
        d_bias_qv,
        d_table,
        joined_proj,
        joined_fc1,
        d_bias_fc1,
        joined_fc2,
        joined_norms,
    )


def solution(mesh):
    in_specs = (
        P(("dp", "tensor"), None),
        P(("dp", "tensor"), None),
        P(None, "dp", None, "tensor"),
        P(None, None, "tensor"),
        P(None, None, "tensor"),
        P(None, "tensor", "dp"),
        P(None, "dp", "tensor"),
        P(None, "tensor"),
        P(None, "tensor", "dp"),
        P(None, None, "dp"),
        P(),
        P(),
        P(),
    )
    out_specs = (
        P(("dp", "tensor"), None),
        P(("dp", "tensor"), None),
        P(None, "dp", None, "tensor"),
        P(None, None, "tensor"),
        P(None, None, "tensor"),
        P(None, "tensor", "dp"),
        P(None, "dp", "tensor"),
        P(None, "tensor"),
        P(None, "tensor", "dp"),
        P(None, None, "dp"),
    )
    return jax.shard_map(body, mesh=mesh, in_specs=in_specs, out_specs=out_specs, check_vma=False)
```

profile of v0, /device:TPU:0, one launch (start us, length us, event | category | flops | bytes accessed | tf_op | source)
XLA Modules:
  0.0 1039.6 jit_solution(14769519194201761679)
XLA Ops:
  11.6 10.8 %all_gather.39 = bf16[2,6,512]{1,0,2:T(2,128)(2,1)S(1)} all-gather(bf16[2,6,64]{1,0,2:T(2,128)(2,1)S(1)} %copy.165), channel_id=1, replica_groups=mesh['dp'=8,'tensor'=4] {'dp'}, dimensions={2}, use_global_device_ids=true | all-gather | bytes 13824 | tf_op jit(solution)/shard_map/all_gather | solution.py:289
  22.8 11.3 %slice_reduce_fusion.6 = (f32[512]{0:T(512)S(1)}, f32[512]{0:T(512)S(1)}, f32[512]{0:T(512)S(1)}, f32[512]{0:T(512)S(1)}, f32[512]{0:T(512)S(1)}, /*index=5*/f32[512]{0:T(512)S(1)}) fusion(f32[1,6,512]{1,0,2:T(1,128)S(1)} %get-tuple-element.115), kind=kLoop, calls=%fused_computation.203 | loop fusion | bytes 24576 | tf_op jit(solution)/shard_map/slice | solution.py:151
  36.9 10.5 %all_gather.41 = bf16[2,512,3,128]{3,0,2,1:T(2,128)(2,1)S(1)} all-gather(bf16[2,64,3,128]{3,0,2,1:T(2,128)(2,1)S(1)} %copy.166), channel_id=1, replica_groups=mesh['dp'=8,'tensor'=4] {'dp'}, dimensions={1}, use_global_device_ids=true | all-gather | bytes 884736 | tf_op jit(solution)/shard_map/all_gather | solution.py:285
  50.5 8.3 all_gather.42
  58.8 14.3 %all-gather.11.cloned.1.call-done = bf16[1568,512]{1,0:T(8,128)(2,1)} async-done(((bf16[392,512]{1,0:T(8,128)(2,1)}), bf16[1568,512]{1,0:T(8,128)(2,1)}) %all-gather.11.cloned.1.call-update) | async-done | bytes 1605648 | tf_op jit(solution)/shard_map/all_gather | solution.py:82
  78.9 3.4 reshape.462
  82.3 2.9 copy.172
  85.2 5.7 squeeze.24
  90.9 5.5 squeeze.25
  108.5 34.3 %reduce-scatter.14.cloned.1.call-done = bf16[392,512]{1,0:T(8,128)(2,1)} async-done(((bf16[1568,512]{1,0:T(8,128)(2,1)}), bf16[392,512]{1,0:T(8,128)(2,1)}) %reduce-scatter.14.cloned.1.call-update) | async-done | bytes 401424 | tf_op jit(solution)/shard_map/reduce_scatter | solution.py:90
  146.5 35.2 %all-gather.13.cloned.1.call-done = bf16[1568,512]{1,0:T(8,128)(2,1)} async-done(((bf16[392,512]{1,0:T(8,128)(2,1)}), bf16[1568,512]{1,0:T(8,128)(2,1)}) %all-gather.13.cloned.1.call-update) | async-done | bytes 1605648 | tf_op jit(solution)/shard_map/all_gather | solution.py:82
  181.7 4.6 multiply_convert_fusion.1
  186.2 19.4 %all-gather.17.cloned.1.call-done = bf16[2,512,512]{1,2,0:T(8,128)(2,1)} async-done(((bf16[2,512,64]{1,2,0:T(8,128)(2,1)}), bf16[2,512,512]{1,2,0:T(8,128)(2,1)}) %all-gather.17.cloned.1.call-update) | async-done | bytes 1048592 | tf_op jit(solution)/shard_map/all_gather | solution.py:288
  205.6 3.2 convolution_convert_fusion.5
  209.3 11.7 %slice_reduce_fusion = (f32[512]{0:T(512)}, f32[512]{0:T(512)}, f32[512]{0:T(512)}, f32[512]{0:T(512)}, f32[512]{0:T(512)S(1)}, /*index=5*/f32[512]{0:T(512)S(1)}) fusion(f32[1,6,512]{1,0,2:T(1,128)S(1)} %get-tuple-element.116), kind=kLoop, calls=%fused_computation.196 | loop fusion | bytes 24576 | tf_op jit(solution)/shard_map/slice | solution.py:151
  221.1 23.9 %reduce-scatter.16.cloned.1.call-done = bf16[392,512]{1,0:T(8,128)(2,1)} async-done(((bf16[1568,512]{1,0:T(8,128)(2,1)}), bf16[392,512]{1,0:T(8,128)(2,1)}) %reduce-scatter.16.cloned.1.call-update) | async-done | bytes 401424 | tf_op jit(solution)/shard_map/reduce_scatter | solution.py:90
  254.3 29.5 %all-gather.19.cloned.1.call-done = bf16[1568,512]{1,0:T(8,128)(2,1)} async-done(((bf16[392,512]{1,0:T(8,128)(2,1)}), bf16[1568,512]{1,0:T(8,128)(2,1)}) %all-gather.19.cloned.1.call-update) | async-done | bytes 1605648 | tf_op jit(solution)/shard_map/all_gather | solution.py:82
  286.3 3.2 copy.177
  289.5 3.5 gather_fusion
  306.7 3.4 reshape.463
  310.1 2.9 copy.184
  313.0 5.7 squeeze.60
  318.7 5.4 squeeze.61
  332.6 3.6 copy.238
  343.9 34.9 %reduce-scatter.18.cloned.1.call-done = bf16[392,512]{1,0:T(8,128)(2,1)} async-done(((bf16[1568,512]{1,0:T(8,128)(2,1)}), bf16[392,512]{1,0:T(8,128)(2,1)}) %reduce-scatter.18.cloned.1.call-update) | async-done | bytes 401424 | tf_op jit(solution)/shard_map/reduce_scatter | solution.py:90
  378.8 3.0 fusion.134
  385.4 35.5 %all-gather.21.cloned.1.call-done = bf16[1568,512]{1,0:T(8,128)(2,1)} async-done(((bf16[392,512]{1,0:T(8,128)(2,1)}), bf16[1568,512]{1,0:T(8,128)(2,1)}) %all-gather.21.cloned.1.call-update) | async-done | bytes 1605648 | tf_op jit(solution)/shard_map/all_gather | solution.py:82
  420.9 5.2 multiply_convert_fusion
  426.1 33.3 %all-gather.23.cloned.1.call-done = bf16[1568,512]{1,0:T(8,128)(2,1)} async-done(((bf16[392,512]{1,0:T(8,128)(2,1)}), bf16[1568,512]{1,0:T(8,128)(2,1)}) %all-gather.23.cloned.1.call-update) | async-done | bytes 1605648 | tf_op jit(solution)/shard_map/all_gather | solution.py:86
  459.3 5.2 fusion.145
  468.0 3.8 convolution_convert_fusion.4
  471.9 31.0 %reduce-scatter.22.cloned.1.call-done = bf16[392,512]{1,0:T(8,128)(2,1)} async-done(((bf16[1568,512]{1,0:T(8,128)(2,1)}), bf16[392,512]{1,0:T(8,128)(2,1)}) %reduce-scatter.22.cloned.1.call-update) | async-done | bytes 401424 | tf_op jit(solution)/shard_map/reduce_scatter | solution.py:99
  506.1 33.7 %reduce-scatter.20.cloned.1.call-done = bf16[392,512]{1,0:T(8,128)(2,1)} async-done(((bf16[1568,512]{1,0:T(8,128)(2,1)}), bf16[392,512]{1,0:T(8,128)(2,1)}) %reduce-scatter.20.cloned.1.call-update) | async-done | bytes 401424 | tf_op jit(solution)/shard_map/reduce_scatter | solution.py:90
  539.8 3.2 fusion.130
  544.9 36.5 %all-gather.25.cloned.1.call-done = bf16[1568,512]{1,0:T(8,128)(2,1)} async-done(((bf16[392,512]{1,0:T(8,128)(2,1)}), bf16[1568,512]{1,0:T(8,128)(2,1)}) %all-gather.25.cloned.1.call-update) | async-done | bytes 1605648 | tf_op jit(solution)/shard_map/all_gather | solution.py:86
  588.4 3.2 copy.194
  591.6 4.0 fusion.141
  604.7 3.4 stack_reshape.20
  608.0 3.0 copy.201
  611.0 3.8 stack_reshape.19
  616.7 2.8 stack_reshape.18
  621.9 4.7 convert_element_type.256
  626.6 3.2 copy.205
  629.8 3.4 gather_fusion.1
  638.2 3.4 convolution_convert_fusion.2
  641.7 34.9 %reduce-scatter.24.cloned.1.call-done = bf16[392,512]{1,0:T(8,128)(2,1)} async-done(((bf16[1568,512]{1,0:T(8,128)(2,1)}), bf16[392,512]{1,0:T(8,128)(2,1)}) %reduce-scatter.24.cloned.1.call-update) | async-done | bytes 401424 | tf_op jit(solution)/shard_map/reduce_scatter | solution.py:99
  682.4 36.3 %all-gather.27.cloned.1.call-done = bf16[1568,512]{1,0:T(8,128)(2,1)} async-done(((bf16[392,512]{1,0:T(8,128)(2,1)}), bf16[1568,512]{1,0:T(8,128)(2,1)}) %all-gather.27.cloned.1.call-update) | async-done | bytes 1605648 | tf_op jit(solution)/shard_map/all_gather | solution.py:86
  718.7 5.2 fusion.146
  727.4 34.9 %reduce-scatter.26.cloned.1.call-done = bf16[392,512]{1,0:T(8,128)(2,1)} async-done(((bf16[1568,512]{1,0:T(8,128)(2,1)}), bf16[392,512]{1,0:T(8,128)(2,1)}) %reduce-scatter.26.cloned.1.call-update) | async-done | bytes 401424 | tf_op jit(solution)/shard_map/reduce_scatter | solution.py:99
  780.2 3.0 fusion.37
  784.4 20.1 %all-gather.29.cloned.1.call-done = bf16[1568,512]{1,0:T(8,128)(2,1)} async-done(((bf16[392,512]{1,0:T(8,128)(2,1)}), bf16[1568,512]{1,0:T(8,128)(2,1)}) %all-gather.29.cloned.1.call-update) | async-done | bytes 1605648 | tf_op jit(solution)/shard_map/all_gather | solution.py:86
  809.6 3.6 reshape.465
  813.2 3.0 copy.208
  817.1 3.3 fusion.143
  822.2 2.8 stack_reshape.23
  825.0 4.5 multiply_reduce_fusion
  833.7 3.6 stack_reshape.22
  845.9 3.6 convolution_convert_fusion
  855.5 23.5 %all-reduce.2 = (f32[2,2,128]{2,1,0:T(2,128)}, f32[2,169,4]{1,2,0:T(4,128)}, f32[2,512]{1,0:T(2,128)}) all-reduce(f32[2,2,128]{2,1,0:T(2,128)S(1)} %pad_maximum_fusion.7, f32[2,169,4]{1,2,0:T(4,128)S(1)} %pad_maximum_fusion.5, f32[2,512]{1,0:T(2,128)S(1)} %pad_maximum_fusion.6), channel_id=1, replica_groups=mesh['dp'=8,'tensor'=4] {'dp'}, use_global_device_ids=true, to_apply=%region_36.38 | all-reduce | flops 2888 | bytes 23104 | tf_op jit(solution)/shard_map/psum | solution.py:353
  879.1 24.2 %all-reduce.7.cloned.1.call-done = (bf16[2,128,512]{1,0,2:T(2,128)(2,1)}, bf16[2,512,512]{1,0,2:T(2,128)(2,1)}) async-done(((bf16[2,128,512]{1,0,2:T(2,128)(2,1)}, bf16[2,512,512]{1,0,2:T(2,128)(2,1)}), (bf16[2,128,512]{1,0,2:T(2,128)(2,1)}, bf16[2,512,512]{1,0,2:T(2,128)(2,1)})) %all-reduce.7.cloned.1.call-update) | async-done | bytes 1310736
  906.4 34.0 %reduce-scatter.30.cloned.1.call-done = bf16[2,64,3,128]{3,1,2,0:T(8,128)(2,1)} async-done(((bf16[2,512,3,128]{3,1,2,0:T(8,128)(2,1)}), bf16[2,64,3,128]{3,1,2,0:T(8,128)(2,1)}) %reduce-scatter.30.cloned.1.call-update) | async-done | bytes 98320 | tf_op jit(solution)/shard_map/reduce_scatter | solution.py:337
  942.0 36.5 %reduce-scatter.28.cloned.1.call-done = bf16[392,512]{1,0:T(8,128)(2,1)} async-done(((bf16[1568,512]{1,0:T(8,128)(2,1)}), bf16[392,512]{1,0:T(8,128)(2,1)}) %reduce-scatter.28.cloned.1.call-update) | async-done | bytes 401424 | tf_op jit(solution)/shard_map/reduce_scatter | solution.py:99
  980.2 17.0 %all-reduce.3 = (bf16[6,512]{1,0:T(8,128)(2,1)S(1)}, bf16[6,512]{1,0:T(8,128)(2,1)S(1)}) all-reduce(f32[6,512]{1,0:T(8,128)S(1)} %stack.87, f32[6,512]{1,0:T(8,128)S(1)} %stack.80), channel_id=1, replica_groups=mesh['dp'=8,'tensor'=4] {'tensor'}, use_global_device_ids=true, to_apply=%region_59.61 | all-reduce | flops 6144 | bytes 36864 | tf_op jit(solution)/shard_map/psum | solution.py:327
  999.5 30.8 %reduce-scatter.34.cloned.1.call-done = bf16[64,12]{1,0:T(8,128)(2,1)} async-done(((bf16[512,12]{1,0:T(8,128)(2,1)}), bf16[64,12]{1,0:T(8,128)(2,1)}) %reduce-scatter.34.cloned.1.call-update) | async-done | bytes 1552
  (433 shorter events, 174.3 us)
Async XLA Ops:
  8.0 26.1 %copy-start.4 = (f32[392,512]{1,0:T(8,128)S(1)}, f32[392,512]{1,0:T(8,128)}, u32[]{:S(2)}) copy-start(f32[392,512]{1,0:T(8,128)} %param.15) | copy-start | bytes 2408452
  8.0 65.1 %all-gather.11.cloned.1.call-start = ((), (), s32[]{:S(2)}) async-start(), calls=%async_computation.11 | async-start | bytes 2007040 | tf_op jit(solution)/shard_map/all_gather | solution.py:82
  10.8 24.2 %copy-start.65 = (f32[392]{0:T(512)}, f32[392]{0:T(512)S(1)}, u32[]{:S(2)}) copy-start(f32[392]{0:T(512)S(1)} %add_rsqrt_fusion.3) | copy-start | bytes 4708
  22.4 12.7 %copy-start.101 = (bf16[2,2,128]{2,1,0:T(2,128)(2,1)S(1)}, bf16[2,2,128]{2,1,0:T(2,128)(2,1)}, u32[]{:S(2)}) copy-start(bf16[2,2,128]{2,1,0:T(2,128)(2,1)} %param.18) | copy-start | bytes 3076
  22.4 13.5 %copy-start.62 = (bf16[2,64,3,128]{3,1,2,0:T(8,128)(2,1)S(1)}, bf16[2,64,3,128]{3,1,2,0:T(8,128)(2,1)}, u32[]{:S(2)}) copy-start(bf16[2,64,3,128]{3,1,2,0:T(8,128)(2,1)} %param.17) | copy-start | bytes 294916
  22.4 13.6 %copy-start.77 = (s32[49,49]{1,0:T(8,128)S(1)}, s32[49,49]{1,0:T(8,128)}, u32[]{:S(2)}) copy-start(s32[49,49]{1,0:T(8,128)} %param.25) | copy-start | bytes 28816
  22.4 13.6 %copy-start.105 = (bf16[2,169,4]{1,2,0:T(4,128)(2,1)S(1)}, bf16[2,169,4]{1,2,0:T(4,128)(2,1)}, u32[]{:S(2)}) copy-start(bf16[2,169,4]{1,2,0:T(4,128)(2,1)} %param.19) | copy-start | bytes 8116
  34.1 110.2 %copy-start.69 = (f32[512]{0:T(512)}, f32[512]{0:T(512)S(1)}, u32[]{:S(2)}) copy-start(f32[512]{0:T(512)S(1)} %get-tuple-element.75) | copy-start | bytes 6148
  35.1 107.8 %reduce-scatter.14.cloned.1.call-start = ((), (), s32[]{:S(2)}) async-start(), calls=%async_computation.12 | async-start | bytes 2007040 | tf_op jit(solution)/shard_map/reduce_scatter | solution.py:90
  36.9 65.0 %copy-start.28 = (f32[4,49,49]{1,2,0:T(8,128)}, f32[4,49,49]{1,2,0:T(8,128)S(1)}, u32[]{:S(2)}) copy-start(f32[4,49,49]{1,2,0:T(8,128)S(1)} %copy.173) | copy-start | bytes 115252
  50.4 25.1 %copy-start.56 = (bf16[1,512,3,128]{1,3,2,0:T(8,128)(2,1)}, bf16[1,512,3,128]{1,3,2,0:T(8,128)(2,1)S(1)}, u32[]{:S(2)}) copy-start(bf16[1,512,3,128]{1,3,2,0:T(8,128)(2,1)S(1)} %copy.250) | copy-start | bytes 1179652
  58.8 47.3 %copy-start.41 = (bf16[2,128,512]{1,2,0:T(8,128)(2,1)}, bf16[2,128,512]{1,2,0:T(8,128)(2,1)S(1)}, u32[]{:S(2)}) copy-start(bf16[2,128,512]{1,2,0:T(8,128)(2,1)S(1)} %all_gather.42) | copy-start | bytes 786436
  85.2 14.0 %copy-start.5 = (bf16[8,4,49,4,32]{2,4,3,1,0:T(8,128)(2,1)}, bf16[8,4,49,4,32]{2,4,3,1,0:T(8,128)(2,1)S(1)}, u32[]{:S(2)}) copy-start(bf16[8,4,49,4,32]{2,4,3,1,0:T(8,128)(2,1)S(1)} %copy.172) | copy-start | bytes 1204228
  106.0 36.8 %copy-start.35 = (bf16[1568,128]{0,1:T(8,128)(2,1)}, bf16[1568,128]{0,1:T(8,128)(2,1)S(1)}, u32[]{:S(2)}) copy-start(bf16[1568,128]{0,1:T(8,128)(2,1)S(1)} %reshape_reshape.7) | copy-start | bytes 1204228
  107.9 38.6 %all-gather.15.cloned.1.call-start = ((), (), s32[]{:S(2)}) async-start(), calls=%async_computation.14 | async-start | bytes 1179648 | tf_op jit(solution)/shard_map/all_gather | solution.py:287
  108.4 73.2 %all-gather.13.cloned.1.call-start = ((), (), s32[]{:S(2)}) async-start(), calls=%async_computation.13 | async-start | bytes 2007040 | tf_op jit(solution)/shard_map/all_gather | solution.py:82
  144.3 37.4 %copy-start.73 = (f32[392]{0:T(512)}, f32[392]{0:T(512)S(1)}, u32[]{:S(2)}) copy-start(f32[392]{0:T(512)S(1)} %add_rsqrt_fusion.2) | copy-start | bytes 4708
  145.3 60.3 %all-gather.17.cloned.1.call-start = ((), (), s32[]{:S(2)}) async-start(), calls=%async_computation.15 | async-start | bytes 1179648 | tf_op jit(solution)/shard_map/all_gather | solution.py:288
  145.9 99.1 %reduce-scatter.16.cloned.1.call-start = ((), (), s32[]{:S(2)}) async-start(), calls=%async_computation.16 | async-start | bytes 2007040 | tf_op jit(solution)/shard_map/reduce_scatter | solution.py:90
  186.2 22.6 %copy-start.47 = (bf16[1568,512]{1,0:T(8,128)(2,1)}, bf16[1568,512]{1,0:T(8,128)(2,1)S(1)}, u32[]{:S(2)}) copy-start(bf16[1568,512]{1,0:T(8,128)(2,1)S(1)} %get-tuple-element.123) | copy-start | bytes 4816900
  208.9 75.0 %all-gather.19.cloned.1.call-start = ((), (), s32[]{:S(2)}) async-start(), calls=%async_computation.17 | async-start | bytes 2007040 | tf_op jit(solution)/shard_map/all_gather | solution.py:82
  221.1 26.4 %copy-start.71 = (f32[512]{0:T(512)}, f32[512]{0:T(512)S(1)}, u32[]{:S(2)}) copy-start(f32[512]{0:T(512)S(1)} %get-tuple-element.72) | copy-start | bytes 6148
  247.5 131.3 %reduce-scatter.18.cloned.1.call-start = ((), (), s32[]{:S(2)}) async-start(), calls=%async_computation.18 | async-start | bytes 2007040 | tf_op jit(solution)/shard_map/reduce_scatter | solution.py:90
  252.3 46.5 %copy-start.39 = (bf16[1,512,3,128]{1,3,2,0:T(8,128)(2,1)}, bf16[1,512,3,128]{1,3,2,0:T(8,128)(2,1)S(1)}, u32[]{:S(2)}) copy-start(bf16[1,512,3,128]{1,3,2,0:T(8,128)(2,1)S(1)} %copy.251) | copy-start | bytes 1179652
  253.7 35.7 %copy-start.81 = (s32[1024]{0:T(1024)}, s32[1024]{0:T(1024)S(1)}, u32[]{:S(2)}) copy-start(s32[1024]{0:T(1024)S(1)} %pad_clamp_fusion.1) | copy-start | bytes 12292
  253.8 84.8 %copy-start.80 = (s32[1024]{0:T(1024)}, s32[1024]{0:T(1024)S(1)}, u32[]{:S(2)}) copy-start(s32[1024]{0:T(1024)S(1)} %pad_clamp_fusion) | copy-start | bytes 12292
  253.8 39.2 %copy-start.99 = (pred[196]{0:T(512)(128)(4,1)}, pred[196]{0:T(512)(128)(4,1)S(1)}, u32[]{:S(2)}) copy-start(pred[196]{0:T(512)(128)(4,1)S(1)} %compare_and_fusion.1) | copy-start | bytes 592
  313.0 14.0 %copy-start.8 = (bf16[8,4,49,4,32]{2,4,3,1,0:T(8,128)(2,1)}, bf16[8,4,49,4,32]{2,4,3,1,0:T(8,128)(2,1)S(1)}, u32[]{:S(2)}) copy-start(bf16[8,4,49,4,32]{2,4,3,1,0:T(8,128)(2,1)S(1)} %copy.184) | copy-start | bytes 1204228
  341.0 37.8 %copy-start.91 = (f32[512]{0:T(512)S(1)}, f32[512]{0:T(512)}, u32[]{:S(2)}) copy-start(f32[512]{0:T(512)} %get-tuple-element.70) | copy-start | bytes 6148
  342.1 36.7 %copy-start.37 = (bf16[1568,128]{1,0:T(8,128)(2,1)}, bf16[1568,128]{1,0:T(8,128)(2,1)S(1)}, u32[]{:S(2)}) copy-start(bf16[1568,128]{1,0:T(8,128)(2,1)S(1)} %reshape.396) | copy-start | bytes 1204228
  343.9 77.0 %all-gather.21.cloned.1.call-start = ((), (), s32[]{:S(2)}) async-start(), calls=%async_computation.19 | async-start | bytes 2007040 | tf_op jit(solution)/shard_map/all_gather | solution.py:82
  384.4 75.0 %all-gather.23.cloned.1.call-start = ((), (), s32[]{:S(2)}) async-start(), calls=%async_computation.21 | async-start | bytes 2007040 | tf_op jit(solution)/shard_map/all_gather | solution.py:86
  384.9 117.9 %reduce-scatter.22.cloned.1.call-start = ((), (), s32[]{:S(2)}) async-start(), calls=%async_computation.22 | async-start | bytes 2007040 | tf_op jit(solution)/shard_map/reduce_scatter | solution.py:99
  459.3 6.3 copy-start.103
  468.0 71.9 %reduce-scatter.20.cloned.1.call-start = ((), (), s32[]{:S(2)}) async-start(), calls=%async_computation.20 | async-start | bytes 2007040 | tf_op jit(solution)/shard_map/reduce_scatter | solution.py:90
  471.8 109.5 %all-gather.25.cloned.1.call-start = ((), (), s32[]{:S(2)}) async-start(), calls=%async_computation.23 | async-start | bytes 2007040 | tf_op jit(solution)/shard_map/all_gather | solution.py:86
  544.8 41.4 %copy-start.100 = (pred[196]{0:T(512)(128)(4,1)S(1)}, pred[196]{0:T(512)(128)(4,1)}, u32[]{:S(2)}) copy-start(pred[196]{0:T(512)(128)(4,1)} %copy-done.99) | copy-start | bytes 592
  544.8 131.8 %reduce-scatter.24.cloned.1.call-start = ((), (), s32[]{:S(2)}) async-start(), calls=%async_computation.24 | async-start | bytes 2007040 | tf_op jit(solution)/shard_map/reduce_scatter | solution.py:99
  626.6 6.6 copy-start.98
  638.2 38.4 %copy-start.72 = (f32[512]{0:T(512)S(1)}, f32[512]{0:T(512)}, u32[]{:S(2)}) copy-start(f32[512]{0:T(512)} %copy-done.71) | copy-start | bytes 6148
  638.2 38.4 %copy-start.76 = (f32[392]{0:T(512)S(1)}, f32[392]{0:T(512)}, u32[]{:S(2)}) copy-start(f32[392]{0:T(512)} %copy-done.75) | copy-start | bytes 4708
  641.6 37.1 %copy-start.22 = (f32[392,512]{1,0:T(8,128)S(1)}, f32[392,512]{1,0:T(8,128)}, u32[]{:S(2)}) copy-start(f32[392,512]{1,0:T(8,128)} %copy-done.21) | copy-start | bytes 2408452
  641.7 77.1 %all-gather.27.cloned.1.call-start = ((), (), s32[]{:S(2)}) async-start(), calls=%async_computation.25 | async-start | bytes 2007040 | tf_op jit(solution)/shard_map/all_gather | solution.py:86
  682.3 80.0 %reduce-scatter.26.cloned.1.call-start = ((), (), s32[]{:S(2)}) async-start(), calls=%async_computation.26 | async-start | bytes 2007040 | tf_op jit(solution)/shard_map/reduce_scatter | solution.py:99
  718.7 6.4 copy-start.104
  725.1 37.2 %copy-start.70 = (f32[512]{0:T(512)S(1)}, f32[512]{0:T(512)}, u32[]{:S(2)}) copy-start(f32[512]{0:T(512)} %copy-done.69) | copy-start | bytes 6148
  725.1 37.2 %copy-start.74 = (f32[392]{0:T(512)S(1)}, f32[392]{0:T(512)}, u32[]{:S(2)}) copy-start(f32[392]{0:T(512)} %copy-done.73) | copy-start | bytes 4708
  727.4 37.1 %copy-start.24 = (f32[392,512]{1,0:T(8,128)S(1)}, f32[392,512]{1,0:T(8,128)}, u32[]{:S(2)}) copy-start(f32[392,512]{1,0:T(8,128)} %copy-done.23) | copy-start | bytes 2408452
  727.4 77.1 %all-gather.29.cloned.1.call-start = ((), (), s32[]{:S(2)}) async-start(), calls=%async_computation.27 | async-start | bytes 2007040 | tf_op jit(solution)/shard_map/all_gather | solution.py:86
  768.1 84.5 %reduce-scatter.32.cloned.1.call-start = ((), (), s32[]{:S(2)}) async-start(), calls=%async_computation.30 | async-start | bytes 1179648 | tf_op jit(solution)/shard_map/reduce_scatter | solution.py:343
  783.2 21.3 %copy-start.36 = (bf16[1568,128]{0,1:T(8,128)(2,1)S(1)}, bf16[1568,128]{0,1:T(8,128)(2,1)}, u32[]{:S(2)}) copy-start(bf16[1568,128]{0,1:T(8,128)(2,1)} %copy-done.35) | copy-start | bytes 1204228
  784.3 23.9 %copy-start.43 = (bf16[2,128,512]{1,2,0:T(8,128)(2,1)S(1)}, bf16[2,128,512]{1,2,0:T(8,128)(2,1)}, u32[]{:S(2)}) copy-start(bf16[2,128,512]{1,2,0:T(8,128)(2,1)} %copy-done.41) | copy-start | bytes 786436
  784.4 118.9 %all-reduce.7.cloned.1.call-start = ((), (), s32[]{:S(2)}) async-start(), calls=%async_computation.32 | async-start | bytes 2621440
  809.6 7.5 copy-start.29
  842.0 98.4 %reduce-scatter.30.cloned.1.call-start = ((), (), s32[]{:S(2)}) async-start(), calls=%async_computation.29 | async-start | bytes 884736 | tf_op jit(solution)/shard_map/reduce_scatter | solution.py:337
  845.8 132.8 %reduce-scatter.28.cloned.1.call-start = ((), (), s32[]{:S(2)}) async-start(), calls=%async_computation.28 | async-start | bytes 2007040 | tf_op jit(solution)/shard_map/reduce_scatter | solution.py:99
  849.6 129.0 %copy-start.64 = (f32[512]{0:T(512)S(1)}, f32[512]{0:T(512)}, u32[]{:S(2)}) copy-start(f32[512]{0:T(512)} %copy-done.63) | copy-start | bytes 6148
  849.6 129.0 %copy-start.66 = (f32[392]{0:T(512)S(1)}, f32[392]{0:T(512)}, u32[]{:S(2)}) copy-start(f32[392]{0:T(512)} %copy-done.65) | copy-start | bytes 4708
  849.6 180.7 %reduce-scatter.34.cloned.1.call-start = ((), (), s32[]{:S(2)}) async-start(), calls=%async_computation.31 | async-start | bytes 147456
  852.5 127.7 %copy-start.86 = (f32[512]{0:T(512)S(1)}, f32[512]{0:T(512)}, u32[]{:S(2)}) copy-start(f32[512]{0:T(512)} %get-tuple-element.63) | copy-start | bytes 6148
  852.5 127.7 %copy-start.93 = (f32[512]{0:T(512)S(1)}, f32[512]{0:T(512)}, u32[]{:S(2)}) copy-start(f32[512]{0:T(512)} %get-tuple-element.90) | copy-start | bytes 6148
  852.5 127.7 %copy-start.94 = (f32[512]{0:T(512)S(1)}, f32[512]{0:T(512)}, u32[]{:S(2)}) copy-start(f32[512]{0:T(512)} %get-tuple-element.92) | copy-start | bytes 6148
  854.6 143.6 %copy-start.20 = (f32[392,512]{1,0:T(8,128)S(1)}, f32[392,512]{1,0:T(8,128)}, u32[]{:S(2)}) copy-start(f32[392,512]{1,0:T(8,128)} %copy-done.19) | copy-start | bytes 2408452
  978.6 19.7 %copy-start.54 = (bf16[392,512]{1,0:T(8,128)(2,1)S(1)}, bf16[392,512]{1,0:T(8,128)(2,1)}, u32[]{:S(2)}) copy-start(bf16[392,512]{1,0:T(8,128)(2,1)} %reduce-scatter.28.cloned.1.call-done) | copy-start | bytes 1204228
  (66 other events, 181.7 us)
Sparse Core Ops, SparseCore 0:
  35.2 37.8 all-gather.10
  108.0 34.7 reduce-scatter.13
  209.0 35.9 reduce-scatter.15
  384.5 36.3 all-gather.20
  422.9 36.4 all-gather.22
  544.9 36.3 all-gather.24
  641.8 34.7 reduce-scatter.23
  727.5 34.8 reduce-scatter.25
Sparse Core Ops, SparseCore 1:
  110.3 22.1 all-gather.14
  145.4 36.2 all-gather.12
  183.5 22.1 all-gather.16
  247.6 36.2 all-gather.18
  344.0 34.8 reduce-scatter.17
  468.0 34.8 reduce-scatter.21
  505.0 34.7 reduce-scatter.19
  682.4 36.3 all-gather.26
  768.2 36.3 all-gather.28
  807.7 34.8 reduce-scatter.31
  845.6 57.6 all-reduce.6
  906.4 34.0 reduce-scatter.29
  942.6 35.9 reduce-scatter.27
  998.3 31.9 reduce-scatter.33
where the time goes:
time: 1050 us; the launch traced here: 1040 us
  waiting for transfers between devices  615 us (59%)
  local copies, waits for them, and re-layouts  177 us (17%)
  matrix products  95.6 us (9%)
  blocking collectives  70.2 us (7%)
  other arithmetic  61.5 us (6%)
  between operations  18.3 us (2%)
    reduce_scatter x4, waiting for transfers between devices, back_sum(): lax.psum_scatter(times_transposed(values, weight).astype(jnp.bfloat16), '...  137 us
    reduce_scatter x4, waiting for transfers between devices, branch_sum(): lax.psum_scatter(jnp.dot(values, weight, preferred_element_type=jnp.float...  127 us
    all_gather x4, waiting for transfers between devices, spread_grads(): return lax.all_gather(values, 'tensor', axis=0, tiled=True)  126 us
    all_gather x4, waiting for transfers between devices, spread_rows(): return lax.all_gather(values, 'tensor', axis=0, tiled=True)  114 us
    unnamed x24, waiting for transfers between devices  56.9 us
    reduce_scatter x1, waiting for transfers between devices, body(): lax.psum_scatter(joined_qkv.astype(jnp.bfloat16), 'dp', scatter_dimension...  34 us
    dot_general x8, matrix products, times_transposed(): lax.dot_general(left_side, right_side, (((1,), (1,)), ((), ())), preferre...  25.2 us
    psum x1, blocking collectives, body(): lax.psum((small_qv, small_table, small_fc1), 'dp')  23.5 us
  transfers between devices with their start and end apart: 22, of which 20 were waited for; matrix products, arithmetic and copies ran while one was open for 11% of the time, Pallas kernels for 0%

commit v1 on v0

--- a/solution.py
+++ b/solution.py
@@ -16,6 +16,22 @@
 full_precision = lax.Precision.HIGHEST
 
 
+def ring_gather(x, axis, dim):
+    ways, here, step = (lax.axis_size(axis), lax.axis_index(axis), x.shape[dim])
+    dims = [n * ways if d == dim else n for d, n in enumerate(x.shape)]
+    full = lax.dynamic_update_slice_in_dim(jnp.zeros(dims, x.dtype), x, here * step, axis=dim)
+    going_up = going_down = x
+    for far in range(1, ways // 2 + 1):
+        going_up = lax.ppermute(going_up, axis, [(d, (d + 1) % ways) for d in range(ways)])
+        full = lax.dynamic_update_slice_in_dim(full, going_up, (here - far) % ways * step, axis=dim)
+        if 2 * far < ways:
+            going_down = lax.ppermute(going_down, axis, [(d, (d - 1) % ways) for d in range(ways)])
+            full = lax.dynamic_update_slice_in_dim(
+                full, going_down, (here + far) % ways * step, axis=dim
+            )
+    return full
+
+
 def gelu_value(inputs):
     return inputs * 0.5 * (1.0 + lax.erf(inputs * ROOT_HALF))
 
@@ -83,7 +99,7 @@
 
 
 def spread_grads(values):
-    return lax.all_gather(values, "tensor", axis=0, tiled=True)
+    return ring_gather(values, "tensor", 0)
 
 
 def branch_sum(values, weight):

time: 1050 us -> 1000 us (0.952)
  waiting for transfers between devices: 615 us -> 538 us
  starting transfers between devices: 1.75 us -> 38.1 us
  matrix products: 95.6 us -> 84.9 us
    all_gather x4 -> x0, waiting for transfers between devices: 126 us -> none  [spread_grads(): return lax.all_gather(values, 'tensor', axis=0, tiled=True)]
    ppermute x0 -> x12, waiting for transfers between devices: none -> 87.6 us  [the longest x8 78.7 us: ring_gather(): lax.ppermute(going_up, axis, [(d, (d + 1) % ways) for d in range(ways)])]
    ppermute x0 -> x12, starting transfers between devices: none -> 36.5 us  [the longest x8 22.8 us: ring_gather(): lax.ppermute(going_up, axis, [(d, (d + 1) % ways) for d in range(ways)])]
    all_gather x4, waiting for transfers between devices: 114 us -> 79.8 us  [spread_rows(): return lax.all_gather(values, 'tensor', axis=0, tiled=True)]
    reduce_scatter x4, waiting for transfers between devices: 127 us -> 139 us  [branch_sum(): lax.psum_scatter(jnp.dot(values, weight, preferred_element_type=jnp.float...]
    unnamed x24 -> x20, waiting for transfers between devices: 56.9 us -> 50.9 us
    slice x2 -> x1, local copies, waits for them, and re-layouts: 23 us -> 21.2 us  [forward_layer(): result = residual + branch_sum(active, w_fc2) + norm_rows[5]]
  transfers between devices with their start and end apart: 22 -> 30, of which waited for: 20 -> 27; matrix products, arithmetic and copies ran while one was open for 11% -> 11% of each run, Pallas kernels for 0% -> 0%
where the time goes in v1:
time: 1000 us; the launch traced here: 995 us
  waiting for transfers between devices  538 us (54%)
  local copies, waits for them, and re-layouts  186 us (19%)
  matrix products  84.9 us (8%)
  blocking collectives  70.2 us (7%)
  other arithmetic  58.9 us (6%)
  starting transfers between devices  38.1 us (4%)
  between operations  18.1 us (2%)
    reduce_scatter x4, waiting for transfers between devices, branch_sum(): lax.psum_scatter(jnp.dot(values, weight, preferred_element_type=jnp.float...  139 us
    reduce_scatter x4, waiting for transfers between devices, back_sum(): lax.psum_scatter(times_transposed(values, weight).astype(jnp.bfloat16), '...  127 us
    all_gather x4, waiting for transfers between devices, spread_rows(): return lax.all_gather(values, 'tensor', axis=0, tiled=True)  79.8 us
    ppermute x8, waiting for transfers between devices, ring_gather(): lax.ppermute(going_up, axis, [(d, (d + 1) % ways) for d in range(ways)])  78.7 us
    unnamed x20, waiting for transfers between devices  50.9 us
    reduce_scatter x1, waiting for transfers between devices, body(): lax.psum_scatter(joined_qkv.astype(jnp.bfloat16), 'dp', scatter_dimension...  34 us
    psum x1, blocking collectives, body(): lax.psum((small_qv, small_table, small_fc1), 'dp')  23.5 us
    ppermute x8, starting transfers between devices, ring_gather(): lax.ppermute(going_up, axis, [(d, (d + 1) % ways) for d in range(ways)])  22.8 us
  transfers between devices with their start and end apart: 30, of which 27 were waited for; matrix products, arithmetic and copies ran while one was open for 11% of the time, Pallas kernels for 0%

profile of v1, /device:TPU:0, one launch (start us, length us, event | category | flops | bytes accessed | tf_op | source)
XLA Modules:
  0.0 994.7 jit_solution(4152438101857558174)
XLA Ops:
  8.9 10.8 %all_gather.27 = bf16[2,6,512]{1,0,2:T(2,128)(2,1)S(1)} all-gather(bf16[2,6,64]{1,0,2:T(2,128)(2,1)S(1)} %copy.165), channel_id=1, replica_groups=mesh['dp'=8,'tensor'=4] {'dp'}, dimensions={2}, use_global_device_ids=true | all-gather | bytes 13824 | tf_op jit(solution)/shard_map/all_gather | solution.py:305
  20.5 21.2 %slice_reduce_fusion = (f32[512]{0:T(512)}, f32[512]{0:T(512)}, f32[512]{0:T(512)}, f32[512]{0:T(512)}, f32[512]{0:T(512)}, /*index=5*/f32[512]{0:T(512)}, f32[5...) fusion(f32[1,6,512]{1,0,2:T(1,128)S(1)} %get-tuple-element.123, ...), kind=kLoop, calls=%fused_computation.196 | loop fusion | bytes 49152 | tf_op jit(solution)/shard_map/slice | solution.py:167
  42.9 10.5 %all_gather.29 = bf16[2,512,3,128]{3,0,2,1:T(2,128)(2,1)S(1)} all-gather(bf16[2,64,3,128]{3,0,2,1:T(2,128)(2,1)S(1)} %copy.166), channel_id=1, replica_groups=mesh['dp'=8,'tensor'=4] {'dp'}, dimensions={1}, use_global_device_ids=true | all-gather | bytes 884736 | tf_op jit(solution)/shard_map/all_gather | solution.py:301
  58.1 8.3 all_gather.30
  66.4 14.3 %all-gather.7.cloned.1.call-done = bf16[1568,512]{1,0:T(8,128)(2,1)} async-done(((bf16[392,512]{1,0:T(8,128)(2,1)}), bf16[1568,512]{1,0:T(8,128)(2,1)}) %all-gather.7.cloned.1.call-update) | async-done | bytes 1605648 | tf_op jit(solution)/shard_map/all_gather | solution.py:98
  85.2 4.9 squeeze.24
  96.9 4.9 squeeze.25
  114.5 34.3 %reduce-scatter.14.cloned.1.call-done = bf16[392,512]{1,0:T(8,128)(2,1)} async-done(((bf16[1568,512]{1,0:T(8,128)(2,1)}), bf16[392,512]{1,0:T(8,128)(2,1)}) %reduce-scatter.14.cloned.1.call-update) | async-done | bytes 401424 | tf_op jit(solution)/shard_map/reduce_scatter | solution.py:106
  153.4 34.8 %all-gather.9.cloned.1.call-done = bf16[1568,512]{1,0:T(8,128)(2,1)} async-done(((bf16[392,512]{1,0:T(8,128)(2,1)}), bf16[1568,512]{1,0:T(8,128)(2,1)}) %all-gather.9.cloned.1.call-update) | async-done | bytes 1605648 | tf_op jit(solution)/shard_map/all_gather | solution.py:98
  188.2 4.6 multiply_convert_fusion.1
  192.7 19.4 %all-gather.13.cloned.1.call-done = bf16[2,512,512]{1,2,0:T(8,128)(2,1)} async-done(((bf16[2,512,64]{1,2,0:T(8,128)(2,1)}), bf16[2,512,512]{1,2,0:T(8,128)(2,1)}) %all-gather.13.cloned.1.call-update) | async-done | bytes 1048592 | tf_op jit(solution)/shard_map/all_gather | solution.py:304
  212.1 3.3 convolution_convert_fusion.5
  215.5 36.1 %reduce-scatter.16.cloned.1.call-done = bf16[392,512]{1,0:T(8,128)(2,1)} async-done(((bf16[1568,512]{1,0:T(8,128)(2,1)}), bf16[392,512]{1,0:T(8,128)(2,1)}) %reduce-scatter.16.cloned.1.call-update) | async-done | bytes 401424 | tf_op jit(solution)/shard_map/reduce_scatter | solution.py:106
  260.6 29.8 %all-gather.15.cloned.1.call-done = bf16[1568,512]{1,0:T(8,128)(2,1)} async-done(((bf16[392,512]{1,0:T(8,128)(2,1)}), bf16[1568,512]{1,0:T(8,128)(2,1)}) %all-gather.15.cloned.1.call-update) | async-done | bytes 1605648 | tf_op jit(solution)/shard_map/all_gather | solution.py:98
  296.0 3.5 gather_fusion
  311.3 4.9 squeeze.60
  316.2 3.4 reshape.463
  325.3 5.4 squeeze.61
  339.2 3.7 copy.238
  350.6 34.9 %reduce-scatter.18.cloned.1.call-done = bf16[392,512]{1,0:T(8,128)(2,1)} async-done(((bf16[1568,512]{1,0:T(8,128)(2,1)}), bf16[392,512]{1,0:T(8,128)(2,1)}) %reduce-scatter.18.cloned.1.call-update) | async-done | bytes 401424 | tf_op jit(solution)/shard_map/reduce_scatter | solution.py:106
  391.7 3.8 collective-permute-start.1
  395.5 15.9 %collective-permute-done = bf16[392,512]{1,0:T(8,128)(2,1)} collective-permute-done((bf16[392,512]{1,0:T(8,128)(2,1)}, bf16[392,512]{1,0:T(8,128)(2,1)}, u32[]{:S(2)}, u32[]{:S(2)}) %collective-permute-start) | collective-permute-done | bytes 401440 | tf_op jit(solution)/shard_map/ppermute | solution.py:25
  411.4 10.4 %collective-permute-start.2 = (bf16[392,512]{1,0:T(8,128)(2,1)}, bf16[392,512]{1,0:T(8,128)(2,1)}, u32[]{:S(2)}, u32[]{:S(2)}) collective-permute-start(bf16[392,512]{1,0:T(8,128)(2,1)} %collective-permute-done), channel_id=1, source_target_pairs={{0,1},{1,2},{2,3},{3,0},{4,5},{5,6},{6,7},{7,4},{8,9},{9,10},{10,1... | collective-permute-start | bytes 1204232 | tf_op jit(solution)/shard_map/ppermute | solution.py:25
  423.6 6.3 collective-permute-done.1
  431.7 12.5 %collective-permute-done.2 = bf16[392,512]{1,0:T(8,128)(2,1)} collective-permute-done((bf16[392,512]{1,0:T(8,128)(2,1)}, bf16[392,512]{1,0:T(8,128)(2,1)}, u32[]{:S(2)}, u32[]{:S(2)}) %collective-permute-start.2) | collective-permute-done | bytes 401440 | tf_op jit(solution)/shard_map/ppermute | solution.py:25
  447.0 4.2 multiply_convert_fusion
  451.2 4.2 fusion.144
  458.9 3.7 convolution_convert_fusion.4
  462.7 31.7 %reduce-scatter.22.cloned.1.call-done = bf16[392,512]{1,0:T(8,128)(2,1)} async-done(((bf16[1568,512]{1,0:T(8,128)(2,1)}), bf16[392,512]{1,0:T(8,128)(2,1)}) %reduce-scatter.22.cloned.1.call-update) | async-done | bytes 401424 | tf_op jit(solution)/shard_map/reduce_scatter | solution.py:115
  497.7 33.8 %reduce-scatter.20.cloned.1.call-done = bf16[392,512]{1,0:T(8,128)(2,1)} async-done(((bf16[1568,512]{1,0:T(8,128)(2,1)}), bf16[392,512]{1,0:T(8,128)(2,1)}) %reduce-scatter.20.cloned.1.call-update) | async-done | bytes 401424 | tf_op jit(solution)/shard_map/reduce_scatter | solution.py:106
  531.5 3.3 fusion.130
  535.2 3.6 collective-permute-start.4
  538.8 10.1 %collective-permute-done.3 = bf16[392,512]{1,0:T(8,128)(2,1)S(1)} collective-permute-done((bf16[392,512]{1,0:T(8,128)(2,1)S(1)}, bf16[392,512]{1,0:T(8,128)(2,1)S(1)}, u32[]{:S(2)}, u32[]{:S(2)}) %collective-permute-start.3) | collective-permute-done | bytes 401440 | tf_op jit(solution)/shard_map/ppermute | solution.py:25
  548.9 4.0 collective-permute-start.5
  554.4 10.2 %collective-permute-done.5 = bf16[392,512]{1,0:T(8,128)(2,1)S(1)} collective-permute-done((bf16[392,512]{1,0:T(8,128)(2,1)S(1)}, bf16[392,512]{1,0:T(8,128)(2,1)S(1)}, u32[]{:S(2)}, u32[]{:S(2)}) %collective-permute-start.5) | collective-permute-done | bytes 401440 | tf_op jit(solution)/shard_map/ppermute | solution.py:25
  574.5 3.4 fusion.140
  586.4 3.4 stack_reshape.20
  592.8 3.6 stack_reshape.19
  603.3 4.7 convert_element_type.256
  608.0 3.2 copy.205
  611.2 3.4 gather_fusion.1
  619.6 3.4 convolution_convert_fusion.2
  623.1 34.1 %reduce-scatter.24.cloned.1.call-done = bf16[392,512]{1,0:T(8,128)(2,1)} async-done(((bf16[1568,512]{1,0:T(8,128)(2,1)}), bf16[392,512]{1,0:T(8,128)(2,1)}) %reduce-scatter.24.cloned.1.call-update) | async-done | bytes 401424 | tf_op jit(solution)/shard_map/reduce_scatter | solution.py:115
  661.2 3.8 collective-permute-start.7
  665.0 10.1 %collective-permute-done.6 = bf16[392,512]{1,0:T(8,128)(2,1)S(1)} collective-permute-done((bf16[392,512]{1,0:T(8,128)(2,1)S(1)}, bf16[392,512]{1,0:T(8,128)(2,1)S(1)}, u32[]{:S(2)}, u32[]{:S(2)}) %collective-permute-start.6) | collective-permute-done | bytes 401440 | tf_op jit(solution)/shard_map/ppermute | solution.py:25
  675.1 4.0 collective-permute-start.8
  680.5 10.2 %collective-permute-done.8 = bf16[392,512]{1,0:T(8,128)(2,1)S(1)} collective-permute-done((bf16[392,512]{1,0:T(8,128)(2,1)S(1)}, bf16[392,512]{1,0:T(8,128)(2,1)S(1)}, u32[]{:S(2)}, u32[]{:S(2)}) %collective-permute-start.8) | collective-permute-done | bytes 401440 | tf_op jit(solution)/shard_map/ppermute | solution.py:25
  696.7 4.0 fusion.40
  706.0 24.8 %reduce-scatter.26.cloned.1.call-done = bf16[392,512]{1,0:T(8,128)(2,1)} async-done(((bf16[1568,512]{1,0:T(8,128)(2,1)}), bf16[392,512]{1,0:T(8,128)(2,1)}) %reduce-scatter.26.cloned.1.call-update) | async-done | bytes 401424 | tf_op jit(solution)/shard_map/reduce_scatter | solution.py:115
  741.6 7.3 collective-permute-done.9
  748.9 3.9 collective-permute-start.11
  753.9 3.7 copy.224
  767.9 4.0 copy.208
  772.0 6.4 multiply_reduce_fusion
  783.0 4.5 fusion.132
  790.3 3.5 stack_reshape.22
  797.7 3.4 stack_reshape.21
  806.7 3.5 convolution_convert_fusion
  816.3 23.5 %all-reduce.2 = (f32[2,2,128]{2,1,0:T(2,128)}, f32[2,169,4]{1,2,0:T(4,128)}, f32[2,512]{1,0:T(2,128)}) all-reduce(f32[2,2,128]{2,1,0:T(2,128)S(1)} %pad_maximum_fusion.7, f32[2,169,4]{1,2,0:T(4,128)S(1)} %pad_maximum_fusion.5, f32[2,512]{1,0:T(2,128)S(1)} %pad_maximum_fusion.6), channel_id=1, replica_groups=mesh['dp'=8,'tensor'=4] {'dp'}, use_global_device_ids=true, to_apply=%region_36.38 | all-reduce | flops 2888 | bytes 23104 | tf_op jit(solution)/shard_map/psum | solution.py:369
  839.8 18.8 %all-reduce.7.cloned.1.call-done = (bf16[2,128,512]{1,0,2:T(2,128)(2,1)}, bf16[2,512,512]{1,0,2:T(2,128)(2,1)}) async-done(((bf16[2,128,512]{1,0,2:T(2,128)(2,1)}, bf16[2,512,512]{1,0,2:T(2,128)(2,1)}), (bf16[2,128,512]{1,0,2:T(2,128)(2,1)}, bf16[2,512,512]{1,0,2:T(2,128)(2,1)})) %all-reduce.7.cloned.1.call-update) | async-done | bytes 1310736
  861.7 34.0 %reduce-scatter.30.cloned.1.call-done = bf16[2,64,3,128]{3,1,2,0:T(8,128)(2,1)} async-done(((bf16[2,512,3,128]{3,1,2,0:T(8,128)(2,1)}), bf16[2,64,3,128]{3,1,2,0:T(8,128)(2,1)}) %reduce-scatter.30.cloned.1.call-update) | async-done | bytes 98320 | tf_op jit(solution)/shard_map/reduce_scatter | solution.py:353
  897.3 36.6 %reduce-scatter.28.cloned.1.call-done = bf16[392,512]{1,0:T(8,128)(2,1)} async-done(((bf16[1568,512]{1,0:T(8,128)(2,1)}), bf16[392,512]{1,0:T(8,128)(2,1)}) %reduce-scatter.28.cloned.1.call-update) | async-done | bytes 401424 | tf_op jit(solution)/shard_map/reduce_scatter | solution.py:115
  935.5 17.0 %all-reduce.3 = (bf16[6,512]{1,0:T(8,128)(2,1)S(1)}, bf16[6,512]{1,0:T(8,128)(2,1)S(1)}) all-reduce(f32[6,512]{1,0:T(8,128)S(1)} %stack.87, f32[6,512]{1,0:T(8,128)S(1)} %stack.80), channel_id=1, replica_groups=mesh['dp'=8,'tensor'=4] {'tensor'}, use_global_device_ids=true, to_apply=%region_59.61 | all-reduce | flops 6144 | bytes 36864 | tf_op jit(solution)/shard_map/psum | solution.py:343
  954.8 30.8 %reduce-scatter.34.cloned.1.call-done = bf16[64,12]{1,0:T(8,128)(2,1)} async-done(((bf16[512,12]{1,0:T(8,128)(2,1)}), bf16[64,12]{1,0:T(8,128)(2,1)}) %reduce-scatter.34.cloned.1.call-update) | async-done | bytes 1552
  (477 shorter events, 208.9 us)
Async XLA Ops:
  8.0 12.1 %copy-start.4 = (f32[392,512]{1,0:T(8,128)S(1)}, f32[392,512]{1,0:T(8,128)}, u32[]{:S(2)}) copy-start(f32[392,512]{1,0:T(8,128)} %param.15) | copy-start | bytes 2408452
  8.0 72.7 %all-gather.7.cloned.1.call-start = ((), (), s32[]{:S(2)}) async-start(), calls=%async_computation.11 | async-start | bytes 2007040 | tf_op jit(solution)/shard_map/all_gather | solution.py:98
  20.5 22.1 %copy-start.73 = (f32[392]{0:T(512)}, f32[392]{0:T(512)S(1)}, u32[]{:S(2)}) copy-start(f32[392]{0:T(512)S(1)} %add_rsqrt_fusion.3) | copy-start | bytes 4708
  20.5 22.2 %copy-start.70 = (bf16[2,64,3,128]{3,1,2,0:T(8,128)(2,1)S(1)}, bf16[2,64,3,128]{3,1,2,0:T(8,128)(2,1)}, u32[]{:S(2)}) copy-start(bf16[2,64,3,128]{3,1,2,0:T(8,128)(2,1)} %param.17) | copy-start | bytes 294916
  41.7 108.6 %copy-start.77 = (f32[512]{0:T(512)}, f32[512]{0:T(512)S(1)}, u32[]{:S(2)}) copy-start(f32[512]{0:T(512)S(1)} %get-tuple-element.155) | copy-start | bytes 6148
  42.7 106.1 %reduce-scatter.14.cloned.1.call-start = ((), (), s32[]{:S(2)}) async-start(), calls=%async_computation.12 | async-start | bytes 2007040 | tf_op jit(solution)/shard_map/reduce_scatter | solution.py:106
  56.4 24.3 %copy-start.63 = (bf16[1,512,3,128]{1,3,2,0:T(8,128)(2,1)}, bf16[1,512,3,128]{1,3,2,0:T(8,128)(2,1)S(1)}, u32[]{:S(2)}) copy-start(bf16[1,512,3,128]{1,3,2,0:T(8,128)(2,1)S(1)} %copy.250) | copy-start | bytes 1179652
  58.0 49.3 %copy-start.28 = (f32[4,49,49]{1,2,0:T(8,128)}, f32[4,49,49]{1,2,0:T(8,128)S(1)}, u32[]{:S(2)}) copy-start(f32[4,49,49]{1,2,0:T(8,128)S(1)} %copy.173) | copy-start | bytes 115252
  66.4 45.6 %copy-start.42 = (bf16[2,128,512]{1,2,0:T(8,128)(2,1)}, bf16[2,128,512]{1,2,0:T(8,128)(2,1)S(1)}, u32[]{:S(2)}) copy-start(bf16[2,128,512]{1,2,0:T(8,128)(2,1)S(1)} %all_gather.30) | copy-start | bytes 786436
  95.1 9.5 copy-start.9
  112.0 36.8 %copy-start.98 = (f32[512]{0:T(512)S(1)}, f32[512]{0:T(512)}, u32[]{:S(2)}) copy-start(f32[512]{0:T(512)} %get-tuple-element.154) | copy-start | bytes 6148
  113.8 39.6 %all-gather.11.cloned.1.call-start = ((), (), s32[]{:S(2)}) async-start(), calls=%async_computation.14 | async-start | bytes 1179648 | tf_op jit(solution)/shard_map/all_gather | solution.py:303
  114.4 73.7 %all-gather.9.cloned.1.call-start = ((), (), s32[]{:S(2)}) async-start(), calls=%async_computation.13 | async-start | bytes 2007040 | tf_op jit(solution)/shard_map/all_gather | solution.py:98
  151.8 60.3 %all-gather.13.cloned.1.call-start = ((), (), s32[]{:S(2)}) async-start(), calls=%async_computation.15 | async-start | bytes 1179648 | tf_op jit(solution)/shard_map/all_gather | solution.py:304
  152.4 99.2 %reduce-scatter.16.cloned.1.call-start = ((), (), s32[]{:S(2)}) async-start(), calls=%async_computation.16 | async-start | bytes 2007040 | tf_op jit(solution)/shard_map/reduce_scatter | solution.py:106
  192.7 22.7 %copy-start.53 = (bf16[1568,512]{1,0:T(8,128)(2,1)}, bf16[1568,512]{1,0:T(8,128)(2,1)S(1)}, u32[]{:S(2)}) copy-start(bf16[1568,512]{1,0:T(8,128)(2,1)S(1)} %get-tuple-element.130) | copy-start | bytes 4816900
  212.1 39.4 %copy-start.97 = (f32[512]{0:T(512)S(1)}, f32[512]{0:T(512)}, u32[]{:S(2)}) copy-start(f32[512]{0:T(512)} %get-tuple-element.157) | copy-start | bytes 6148
  215.4 37.6 %copy-start.79 = (f32[512]{0:T(512)S(1)}, f32[512]{0:T(512)}, u32[]{:S(2)}) copy-start(f32[512]{0:T(512)} %get-tuple-element.72) | copy-start | bytes 6148
  215.4 37.7 %copy-start.90 = (f32[512]{0:T(512)S(1)}, f32[512]{0:T(512)}, u32[]{:S(2)}) copy-start(f32[512]{0:T(512)} %get-tuple-element.71) | copy-start | bytes 6148
  215.4 75.0 %all-gather.15.cloned.1.call-start = ((), (), s32[]{:S(2)}) async-start(), calls=%async_computation.17 | async-start | bytes 2007040 | tf_op jit(solution)/shard_map/all_gather | solution.py:98
  254.0 131.4 %reduce-scatter.18.cloned.1.call-start = ((), (), s32[]{:S(2)}) async-start(), calls=%async_computation.18 | async-start | bytes 2007040 | tf_op jit(solution)/shard_map/reduce_scatter | solution.py:106
  256.3 49.1 %copy-start.39 = (bf16[1,512,3,128]{1,3,2,0:T(8,128)(2,1)}, bf16[1,512,3,128]{1,3,2,0:T(8,128)(2,1)S(1)}, u32[]{:S(2)}) copy-start(bf16[1,512,3,128]{1,3,2,0:T(8,128)(2,1)S(1)} %copy.251) | copy-start | bytes 1179652
  260.1 35.9 %copy-start.89 = (s32[1024]{0:T(1024)}, s32[1024]{0:T(1024)S(1)}, u32[]{:S(2)}) copy-start(s32[1024]{0:T(1024)S(1)} %pad_clamp_fusion.1) | copy-start | bytes 12292
  260.1 85.1 %copy-start.88 = (s32[1024]{0:T(1024)}, s32[1024]{0:T(1024)S(1)}, u32[]{:S(2)}) copy-start(s32[1024]{0:T(1024)S(1)} %pad_clamp_fusion) | copy-start | bytes 12292
  260.6 38.9 %copy-start.101 = (pred[196]{0:T(512)(128)(4,1)}, pred[196]{0:T(512)(128)(4,1)S(1)}, u32[]{:S(2)}) copy-start(pred[196]{0:T(512)(128)(4,1)S(1)} %get-tuple-element.161) | copy-start | bytes 592
  322.5 11.0 %copy-start.11 = (bf16[8,4,49,4,32]{2,4,3,1,0:T(8,128)(2,1)}, bf16[8,4,49,4,32]{2,4,3,1,0:T(8,128)(2,1)S(1)}, u32[]{:S(2)}) copy-start(bf16[8,4,49,4,32]{2,4,3,1,0:T(8,128)(2,1)S(1)} %copy.184) | copy-start | bytes 1204228
  348.7 36.7 %copy-start.96 = (f32[512]{0:T(512)S(1)}, f32[512]{0:T(512)}, u32[]{:S(2)}) copy-start(f32[512]{0:T(512)} %get-tuple-element.70) | copy-start | bytes 6148
  350.5 96.5 %all-gather.17.cloned.1.call-start = ((), (), s32[]{:S(2)}) async-start(), calls=%async_computation.19 | async-start | bytes 2007040 | tf_op jit(solution)/shard_map/all_gather | solution.py:98
  389.2 105.2 %reduce-scatter.22.cloned.1.call-start = ((), (), s32[]{:S(2)}) async-start(), calls=%async_computation.21 | async-start | bytes 2007040 | tf_op jit(solution)/shard_map/reduce_scatter | solution.py:115
  391.6 19.8 %collective-permute-start = (bf16[392,512]{1,0:T(8,128)(2,1)}, bf16[392,512]{1,0:T(8,128)(2,1)}, u32[]{:S(2)}, u32[]{:S(2)}) collective-permute-start(bf16[392,512]{1,0:T(8,128)(2,1)} %get-tuple-element.107), channel_id=1, source_target_pairs={{0,1},{1,2},{2,3},{3,0},{4,5},{5,6},{6,7},{7,4},{8,9},{9,10},{10,1... | collective-permute-start | bytes 1204232 | tf_op jit(solution)/shard_map/ppermute | solution.py:25
  391.7 38.2 %collective-permute-start.1 = (bf16[392,512]{1,0:T(8,128)(2,1)}, bf16[392,512]{1,0:T(8,128)(2,1)}, u32[]{:S(2)}, u32[]{:S(2)}) collective-permute-start(bf16[392,512]{1,0:T(8,128)(2,1)} %get-tuple-element.107), channel_id=1, source_target_pairs={{0,3},{1,0},{2,1},{3,2},{4,7},{5,4},{6,5},{7,6},{8,11},{9,8},{10,9... | collective-permute-start | bytes 1204232 | tf_op jit(solution)/shard_map/ppermute | solution.py:28
  411.4 32.8 %collective-permute-start.2 = (bf16[392,512]{1,0:T(8,128)(2,1)}, bf16[392,512]{1,0:T(8,128)(2,1)}, u32[]{:S(2)}, u32[]{:S(2)}) collective-permute-start(bf16[392,512]{1,0:T(8,128)(2,1)} %collective-permute-done), channel_id=1, source_target_pairs={{0,1},{1,2},{2,3},{3,0},{4,5},{5,6},{6,7},{7,4},{8,9},{9,10},{10,1... | collective-permute-start | bytes 1204232 | tf_op jit(solution)/shard_map/ppermute | solution.py:25
  458.9 72.6 %reduce-scatter.20.cloned.1.call-start = ((), (), s32[]{:S(2)}) async-start(), calls=%async_computation.20 | async-start | bytes 2007040 | tf_op jit(solution)/shard_map/reduce_scatter | solution.py:106
  462.7 194.6 %reduce-scatter.24.cloned.1.call-start = ((), (), s32[]{:S(2)}) async-start(), calls=%async_computation.22 | async-start | bytes 2007040 | tf_op jit(solution)/shard_map/reduce_scatter | solution.py:115
  534.7 18.2 %copy-start.24 = (f32[392,512]{1,0:T(8,128)}, f32[392,512]{1,0:T(8,128)S(1)}, u32[]{:S(2)}) copy-start(f32[392,512]{1,0:T(8,128)S(1)} %get-tuple-element.95) | copy-start | bytes 2408452
  534.9 14.0 %collective-permute-start.3 = (bf16[392,512]{1,0:T(8,128)(2,1)S(1)}, bf16[392,512]{1,0:T(8,128)(2,1)S(1)}, u32[]{:S(2)}, u32[]{:S(2)}) collective-permute-start(bf16[392,512]{1,0:T(8,128)(2,1)S(1)} %get-tuple-element.105), channel_id=1, source_target_pairs={{0,1},{1,2},{2,3},{3,0},{4,5},{5,6},{6,7},{7,4},{8,9},{9,10},{10,1... | collective-permute-start | bytes 1204232 | tf_op jit(solution)/shard_map/ppermute | solution.py:25
  535.2 19.2 %collective-permute-start.4 = (bf16[392,512]{1,0:T(8,128)(2,1)S(1)}, bf16[392,512]{1,0:T(8,128)(2,1)S(1)}, u32[]{:S(2)}, u32[]{:S(2)}) collective-permute-start(bf16[392,512]{1,0:T(8,128)(2,1)S(1)} %get-tuple-element.105), channel_id=1, source_target_pairs={{0,3},{1,0},{2,1},{3,2},{4,7},{5,4},{6,5},{7,6},{8,11},{9,8},{10,9... | collective-permute-start | bytes 1204232 | tf_op jit(solution)/shard_map/ppermute | solution.py:28
  548.9 15.7 %collective-permute-start.5 = (bf16[392,512]{1,0:T(8,128)(2,1)S(1)}, bf16[392,512]{1,0:T(8,128)(2,1)S(1)}, u32[]{:S(2)}, u32[]{:S(2)}) collective-permute-start(bf16[392,512]{1,0:T(8,128)(2,1)S(1)} %collective-permute-done.3), channel_id=1, source_target_pairs={{0,1},{1,2},{2,3},{3,0},{4,5},{5,6},{6,7},{7,4},{8,9},{9,10},{10,1... | collective-permute-start | bytes 1204232 | tf_op jit(solution)/shard_map/ppermute | solution.py:25
  619.6 37.7 %copy-start.80 = (f32[512]{0:T(512)S(1)}, f32[512]{0:T(512)}, u32[]{:S(2)}) copy-start(f32[512]{0:T(512)} %get-tuple-element.72) | copy-start | bytes 6148
  619.6 37.7 %copy-start.84 = (f32[392]{0:T(512)S(1)}, f32[392]{0:T(512)}, u32[]{:S(2)}) copy-start(f32[392]{0:T(512)} %copy-done.83) | copy-start | bytes 4708
  623.1 107.7 %reduce-scatter.26.cloned.1.call-start = ((), (), s32[]{:S(2)}) async-start(), calls=%async_computation.23 | async-start | bytes 2007040 | tf_op jit(solution)/shard_map/reduce_scatter | solution.py:115
  660.9 29.9 %copy-start.116 = (f32[1568,512]{1,0:T(8,128)S(1)}, f32[1568,512]{1,0:T(8,128)}, u32[]{:S(2)}) copy-start(f32[1568,512]{1,0:T(8,128)} %get-tuple-element.131) | copy-start | bytes 9633796
  661.0 29.8 %copy-start.112 = (bf16[2,512,512]{1,2,0:T(8,128)(2,1)S(1)}, bf16[2,512,512]{1,2,0:T(8,128)(2,1)}, u32[]{:S(2)}) copy-start(bf16[2,512,512]{1,2,0:T(8,128)(2,1)} %all-gather.13.cloned.1.call-done) | copy-start | bytes 3145732
  661.1 14.0 %collective-permute-start.6 = (bf16[392,512]{1,0:T(8,128)(2,1)S(1)}, bf16[392,512]{1,0:T(8,128)(2,1)S(1)}, u32[]{:S(2)}, u32[]{:S(2)}) collective-permute-start(bf16[392,512]{1,0:T(8,128)(2,1)S(1)} %get-tuple-element.103), channel_id=1, source_target_pairs={{0,1},{1,2},{2,3},{3,0},{4,5},{5,6},{6,7},{7,4},{8,9},{9,10},{10,1... | collective-permute-start | bytes 1204232 | tf_op jit(solution)/shard_map/ppermute | solution.py:25
  661.2 19.2 %collective-permute-start.7 = (bf16[392,512]{1,0:T(8,128)(2,1)S(1)}, bf16[392,512]{1,0:T(8,128)(2,1)S(1)}, u32[]{:S(2)}, u32[]{:S(2)}) collective-permute-start(bf16[392,512]{1,0:T(8,128)(2,1)S(1)} %get-tuple-element.103), channel_id=1, source_target_pairs={{0,3},{1,0},{2,1},{3,2},{4,7},{5,4},{6,5},{7,6},{8,11},{9,8},{10,9... | collective-permute-start | bytes 1204232 | tf_op jit(solution)/shard_map/ppermute | solution.py:28
  675.1 15.6 %collective-permute-start.8 = (bf16[392,512]{1,0:T(8,128)(2,1)S(1)}, bf16[392,512]{1,0:T(8,128)(2,1)S(1)}, u32[]{:S(2)}, u32[]{:S(2)}) collective-permute-start(bf16[392,512]{1,0:T(8,128)(2,1)S(1)} %collective-permute-done.6), channel_id=1, source_target_pairs={{0,1},{1,2},{2,3},{3,0},{4,5},{5,6},{6,7},{7,4},{8,9},{9,10},{10,1... | collective-permute-start | bytes 1204232 | tf_op jit(solution)/shard_map/ppermute | solution.py:25
  696.6 116.6 %reduce-scatter.32.cloned.1.call-start = ((), (), s32[]{:S(2)}) async-start(), calls=%async_computation.26 | async-start | bytes 1179648 | tf_op jit(solution)/shard_map/reduce_scatter | solution.py:359
  704.1 26.7 %copy-start.78 = (f32[512]{0:T(512)S(1)}, f32[512]{0:T(512)}, u32[]{:S(2)}) copy-start(f32[512]{0:T(512)} %copy-done.77) | copy-start | bytes 6148
  704.1 26.7 %copy-start.82 = (f32[392]{0:T(512)S(1)}, f32[392]{0:T(512)}, u32[]{:S(2)}) copy-start(f32[392]{0:T(512)} %copy-done.81) | copy-start | bytes 4708
  734.6 14.3 %collective-permute-start.9 = (bf16[392,512]{1,0:T(8,128)(2,1)}, bf16[392,512]{1,0:T(8,128)(2,1)}, u32[]{:S(2)}, u32[]{:S(2)}) collective-permute-start(bf16[392,512]{1,0:T(8,128)(2,1)} %get-tuple-element.101), channel_id=1, source_target_pairs={{0,1},{1,2},{2,3},{3,0},{4,5},{5,6},{6,7},{7,4},{8,9},{9,10},{10,1... | collective-permute-start | bytes 1204232 | tf_op jit(solution)/shard_map/ppermute | solution.py:25
  737.1 15.7 %copy-start.46 = (bf16[1,512,512]{2,1,0:T(8,128)(2,1)S(1)}, bf16[1,512,512]{2,1,0:T(8,128)(2,1)}, u32[]{:S(2)}) copy-start(bf16[1,512,512]{2,1,0:T(8,128)(2,1)} %fusion.40) | copy-start | bytes 1572868
  737.1 24.2 %collective-permute-start.10 = (bf16[392,512]{1,0:T(8,128)(2,1)}, bf16[392,512]{1,0:T(8,128)(2,1)}, u32[]{:S(2)}, u32[]{:S(2)}) collective-permute-start(bf16[392,512]{1,0:T(8,128)(2,1)} %get-tuple-element.101), channel_id=1, source_target_pairs={{0,3},{1,0},{2,1},{3,2},{4,7},{5,4},{6,5},{7,6},{8,11},{9,8},{10,9... | collective-permute-start | bytes 1204232 | tf_op jit(solution)/shard_map/ppermute | solution.py:28
  741.6 16.0 %copy-start.45 = (bf16[1,512,512]{2,1,0:T(8,128)(2,1)S(1)}, bf16[1,512,512]{2,1,0:T(8,128)(2,1)}, u32[]{:S(2)}) copy-start(bf16[1,512,512]{2,1,0:T(8,128)(2,1)} %fusion.38) | copy-start | bytes 1572868
  748.9 15.6 %collective-permute-start.11 = (bf16[392,512]{1,0:T(8,128)(2,1)}, bf16[392,512]{1,0:T(8,128)(2,1)}, u32[]{:S(2)}, u32[]{:S(2)}) collective-permute-start(bf16[392,512]{1,0:T(8,128)(2,1)} %collective-permute-done.9), channel_id=1, source_target_pairs={{0,1},{1,2},{2,3},{3,0},{4,5},{5,6},{6,7},{7,4},{8,9},{9,10},{10,1... | collective-permute-start | bytes 1204232 | tf_op jit(solution)/shard_map/ppermute | solution.py:25
  759.8 98.7 %all-reduce.7.cloned.1.call-start = ((), (), s32[]{:S(2)}) async-start(), calls=%async_computation.28 | async-start | bytes 2621440
  771.9 6.4 copy-start.15
  802.5 93.3 %reduce-scatter.30.cloned.1.call-start = ((), (), s32[]{:S(2)}) async-start(), calls=%async_computation.25 | async-start | bytes 884736 | tf_op jit(solution)/shard_map/reduce_scatter | solution.py:353
  806.6 127.3 %reduce-scatter.28.cloned.1.call-start = ((), (), s32[]{:S(2)}) async-start(), calls=%async_computation.24 | async-start | bytes 2007040 | tf_op jit(solution)/shard_map/reduce_scatter | solution.py:115
  810.3 175.2 %reduce-scatter.34.cloned.1.call-start = ((), (), s32[]{:S(2)}) async-start(), calls=%async_computation.27 | async-start | bytes 147456
  812.2 121.7 %copy-start.72 = (f32[512]{0:T(512)S(1)}, f32[512]{0:T(512)}, u32[]{:S(2)}) copy-start(f32[512]{0:T(512)} %copy-done.71) | copy-start | bytes 6148
  812.2 121.7 %copy-start.74 = (f32[392]{0:T(512)S(1)}, f32[392]{0:T(512)}, u32[]{:S(2)}) copy-start(f32[392]{0:T(512)} %copy-done.73) | copy-start | bytes 4708
  815.2 120.3 %copy-start.99 = (f32[512]{0:T(512)S(1)}, f32[512]{0:T(512)}, u32[]{:S(2)}) copy-start(f32[512]{0:T(512)} %get-tuple-element.90) | copy-start | bytes 6148
  816.2 137.3 %copy-start.23 = (f32[392,512]{1,0:T(8,128)S(1)}, f32[392,512]{1,0:T(8,128)}, u32[]{:S(2)}) copy-start(f32[392,512]{1,0:T(8,128)} %copy-done.22) | copy-start | bytes 2408452
  933.9 19.7 %copy-start.60 = (bf16[392,512]{1,0:T(8,128)(2,1)S(1)}, bf16[392,512]{1,0:T(8,128)(2,1)}, u32[]{:S(2)}) copy-start(bf16[392,512]{1,0:T(8,128)(2,1)} %reduce-scatter.28.cloned.1.call-done) | copy-start | bytes 1204228
  (83 other events, 249.6 us)
Sparse Core Ops, SparseCore 0:
  42.8 37.8 all-gather.6
  114.0 34.7 reduce-scatter.13
  215.5 35.9 reduce-scatter.15
  389.3 57.6 all-gather.16
  459.0 35.4 reduce-scatter.21
  496.6 34.8 reduce-scatter.19
Sparse Core Ops, SparseCore 1:
  116.2 22.1 all-gather.10
  151.9 36.2 all-gather.8
  189.9 22.1 all-gather.12
  254.1 36.2 all-gather.14
  350.6 34.8 reduce-scatter.17
  623.2 34.1 reduce-scatter.23
  696.7 34.1 reduce-scatter.25
  759.9 36.4 reduce-scatter.31
  802.6 55.9 all-reduce.6
  861.7 34.0 reduce-scatter.29
  897.9 35.9 reduce-scatter.27
  953.6 31.9 reduce-scatter.33
